TPU v7x, 256 devices: a whole 4x4x8 slice. The times are simulated.
256 devices in a mesh: row: 16 (over z, core), col: 16 (over x, y).
Axes of the slice: x: 4, y: 4, z: 8, core: 2. Of those that a mesh axis runs over, the one named last changes fastest.
Arguments:
- work: float32 [8192, 8192], P('row', 'col'), may hold values from -6 to 6
- a_tiles: bfloat16 [16, 16, 512, 512], P('row', None, 'col'), may hold values from -0.078125 to 0.078125
- b_tiles: bfloat16 [16, 16, 512, 512], P(None, 'col', 'row'), may hold values from -0.078125 to 0.078125
- u_powers: float32 [16, 3, 512, 512], P('row', None, 'col'), may hold values from -1 to 1, as said below
- v_powers: float32 [16, 3, 512, 512], P('col', None, 'row'), may hold values from -1 to 1, as said below
- shift: float32 [1], replicated, may hold values from 0.5 to 2
Outputs:
- progress: float32 [8192, 8192], P('row', 'col')
Inputs may be any that keep to these rules, and one draw needn't show every extreme that they name: u_powers[i] holds U, U^2 and U^4 for a lower triangular U whose diagonal entries have magnitudes 0.3 to 0.9. v_powers[j] holds V, V^2 and V^4 for an upper triangular V whose diagonal entries have magnitudes 0.3 to 0.9.
All inputs are finite; a program needn't handle non-finite values.
Results may differ from a plain program's by a relative error of at most 0.0023.
Values may be sent and summed in bfloat16 or wider, within the bound.
No kernel may reach another device: no remote copies, remote signals or barrier semaphores. Data moves between devices by JAX's collectives and lax.ppermute only.
A program may use at most 128 MiB of HBM per device.

v0:
```python
import jax
import jax.numpy as jnp
import numpy as np
from jax import lax
from jax.sharding import PartitionSpec as P

FRONTS = 3
finest = lax.Precision.HIGHEST


def in_order(blocks, dim):
    blocks = jnp.moveaxis(blocks, 0, dim)
    shape = blocks.shape
    return blocks.reshape(*shape[:dim], shape[dim] * shape[dim + 1], *shape[dim + 2 :])


def from_everyone(array, axis):
    copies = jnp.broadcast_to(array, (lax.axis_size(axis), *array.shape))
    return lax.all_to_all(copies, axis, split_axis=0, concat_axis=0, tiled=True)


def gathered_copies(array, axis, dim):
    return in_order(from_everyone(array, axis), dim)


def broadcast(array, axis, root):
    return lax.dynamic_index_in_dim(lax.all_gather(array, axis), root, 0, keepdims=False)


def product(left_side, right_side):
    return jnp.dot(left_side, right_side, preferred_element_type=jnp.float32, precision=finest)


def keep(source):
    return source


def per_device(work, a_tiles, b_tiles, u_powers, v_powers, shift):
    rows_count = lax.axis_size("row")
    cols_count = lax.axis_size("col")
    my_row = lax.axis_index("row")
    my_col = lax.axis_index("col")
    my_front = my_row + my_col
    first = max(0, (rows_count + cols_count) // 2 - FRONTS)
    width = work.shape[0]
    identity = jnp.eye(width, dtype=jnp.float32)
    shift_value = shift[0]
    u_base = gathered_copies(u_powers[:, :1], "col", 2)[0, 0]
    v_base = lax.all_gather(v_powers[:, :1], "row", axis=2, tiled=True)[0, 0]

    def powers_of():
        u_square = product(u_base, u_base)
        v_square = product(v_base, v_base)
        return (
            [u_base, u_square, product(u_square, u_square)],
            [v_base, v_square, product(v_square, v_square)],
        )

    def solve(source):
        u_list, v_list = powers_of()
        current = product(product(identity - u_list[0], source), identity - v_list[0]) / (
            2.0 * shift_value
        )
        for power in range(3):
            current = current + product(product(u_list[power], current), v_list[power])
        return current

    current = work
    for number in range(FRONTS):
        front = first + number
        current = lax.cond(my_front == front, solve, keep, current)
        sent = current.astype(jnp.bfloat16)
        down_row = front - my_col
        across_col = front - my_row
        valid_down = (down_row >= 0) & (down_row < rows_count)
        valid_across = (across_col >= 0) & (across_col < cols_count)
        down_clip = jnp.clip(down_row, 0, rows_count - 1)
        across_clip = jnp.clip(across_col, 0, cols_count - 1)
        down_tile = broadcast(sent, "row", down_clip)
        across_tile = broadcast(sent, "col", across_clip)
        a_rows = np.clip(front - np.arange(cols_count), 0, rows_count - 1).astype(np.int32)
        b_rows = np.clip(front - np.arange(rows_count), 0, cols_count - 1).astype(np.int32)
        a_tile = lax.all_to_all(
            a_tiles[0, a_rows], "col", split_axis=0, concat_axis=0, tiled=True
        ).reshape(width, width)
        b_tile = lax.all_to_all(
            b_tiles[b_rows, 0], "row", split_axis=0, concat_axis=0, tiled=True
        ).reshape(width, width)

        def update(source):
            minus_a = jnp.dot(a_tile, down_tile, preferred_element_type=jnp.float32)
            minus_b = jnp.dot(across_tile, b_tile, preferred_element_type=jnp.float32)
            return (
                source - jnp.where(valid_down, minus_a, 0.0) - jnp.where(valid_across, minus_b, 0.0)
            )

        current = lax.cond(my_front > front, update, keep, current)
    return current


def solution(mesh):
    placed = (
        P("row", "col"),
        P("row", None, "col", None),
        P(None, "col", "row", None),
        P("row", None, "col", None),
        P("col", None, "row", None),
        P(),
    )
    return jax.shard_map(
        per_device, mesh=mesh, in_specs=placed, out_specs=P("row", "col"), check_vma=False
    )
```

profile of v0, /device:TPU:70, one launch (start us, length us, event | category | flops | bytes accessed | tf_op | source)
XLA Modules:
  0.0 593.5 jit_solution(3004908231699741183)
XLA Ops:
  6.5 2.3 copy.78
  8.9 1.5 slice.10
  10.3 0.0 all-gather.14.cloned.1.call-update
  10.4 0.8 slice_bitcast_fusion
  11.2 1.1 broadcast_in_dim.35
  12.3 7.4 %all-to-all-start = ((f32[16,1,1,32,512]{4,3,2,1,0:T(8,128)}), f32[16,1,1,32,512]{4,3,2,1,0:T(8,128)S(1)}, u32[]{:S(2)}, u32[]{:S(2)}) async-start(f32[16,1,1,32,512]{4,3,2,1,0:T(8,128)} %broadcast_in_dim.35), calls=%async_computation | async-start | bytes 2097152 | tf_op jit(solution)/shard_map/all_to_all | solution.py:19
  19.8 0.0 all-gather.18.cloned.1.call-start
  19.8 1.1 fusion.36
  20.9 14.1 %all-to-all-done = f32[16,1,1,32,512]{4,3,2,1,0:T(8,128)S(1)} async-done(((f32[16,1,1,32,512]{4,3,2,1,0:T(8,128)}), f32[16,1,1,32,512]{4,3,2,1,0:T(8,128)S(1)}, u32[]{:S(2)}, u32[]{:S(2)}) %all-to-all-start) | async-done | bytes 1048608 | tf_op jit(solution)/shard_map/all_to_all | solution.py:19
  35.0 14.5 %all-gather.14.cloned.1.call-done = f32[1,1,512,512]{3,2,1,0:T(8,128)} async-done(((f32[1,1,32,512]{3,2,1,0:T(8,128)}), f32[1,1,512,512]{3,2,1,0:T(8,128)}) %all-gather.14.cloned.1.call-update) | async-done | bytes 1048592 | tf_op jit(solution)/shard_map/all_gather | solution.py:49
  49.5 2.9 conditional.6
  52.4 2.2 convert_element_type.47
  54.6 0.0 all-gather.18.cloned.1.call-update
  54.6 0.0 all-gather.16.cloned.1.call-start
  54.6 0.7 all-gather.16.cloned.1.call-update
  55.3 1.4 gather_fusion
  56.7 33.7 %all-to-all-start.1 = ((bf16[16,32,512]{2,1,0:T(8,128)(2,1)}), bf16[16,32,512]{2,1,0:T(8,128)(2,1)}, u32[]{:S(2)}, u32[]{:S(2)}) async-start(bf16[16,32,512]{2,1,0:T(8,128)(2,1)} %gather_fusion), calls=%async_computation.1 | async-start | bytes 1048576 | tf_op jit(solution)/shard_map/all_to_all | solution.py:83
  90.4 1.4 gather_fusion.1
  91.8 8.6 %all-to-all-done.1 = bf16[16,32,512]{2,1,0:T(8,128)(2,1)} async-done(((bf16[16,32,512]{2,1,0:T(8,128)(2,1)}), bf16[16,32,512]{2,1,0:T(8,128)(2,1)}, u32[]{:S(2)}, u32[]{:S(2)}) %all-to-all-start.1) | async-done | bytes 524320 | tf_op jit(solution)/shard_map/all_to_all | solution.py:83
  100.4 10.2 %all-to-all-start.2 = ((bf16[16,32,512]{2,1,0:T(8,128)(2,1)}), bf16[16,32,512]{2,1,0:T(8,128)(2,1)}, u32[]{:S(2)}, u32[]{:S(2)}) async-start(bf16[16,32,512]{2,1,0:T(8,128)(2,1)} %gather_fusion.1), calls=%async_computation.2 | async-start | bytes 1048576 | tf_op jit(solution)/shard_map/all_to_all | solution.py:86
  110.6 0.0 all-gather.20.cloned.1.call-start
  110.6 14.9 %all-to-all-done.2 = bf16[16,32,512]{2,1,0:T(8,128)(2,1)} async-done(((bf16[16,32,512]{2,1,0:T(8,128)(2,1)}), bf16[16,32,512]{2,1,0:T(8,128)(2,1)}, u32[]{:S(2)}, u32[]{:S(2)}) %all-to-all-start.2) | async-done | bytes 524320 | tf_op jit(solution)/shard_map/all_to_all | solution.py:86
  125.5 31.5 %all-gather.18.cloned.1.call-done = bf16[8192,512]{1,0:T(8,128)(2,1)} async-done(((bf16[512,512]{1,0:T(8,128)(2,1)}), bf16[8192,512]{1,0:T(8,128)(2,1)}) %all-gather.18.cloned.1.call-update) | async-done | bytes 8388624 | tf_op jit(solution)/shard_map/all_gather | solution.py:27
  156.9 55.6 %all-gather.16.cloned.1.call-done = bf16[8192,512]{1,0:T(8,128)(2,1)} async-done(((bf16[512,512]{1,0:T(8,128)(2,1)}), bf16[8192,512]{1,0:T(8,128)(2,1)}) %all-gather.16.cloned.1.call-update) | async-done | bytes 8388624 | tf_op jit(solution)/shard_map/all_gather | solution.py:27
  212.6 8.5 %conditional.7 = (f32[512,512]{0,1:T(8,128)}) conditional(s32[]{:T(128)} %convert_element_type.44, (f32[512,512]{1,0:T(8,128)}) %conditional.6, (s32[]{:T(128)}, bf16[16,32,512]{2,1,0:T(8,128)(2,1)}, bf16[16,512,512]{2,1,0:T(8,128)(2,1)}, f32[512,512]{1,0:T(8,128)}, s32[]{:T(128)}, /*index=5*/bf16[16,512,512]{2,1,0:T(8,128)(2,1)}, ...), branch_computations={%region_2.3_spmd, %region_3.4_spmd.clone} | conditional | flops 537919488 | bytes 8388740 | solution.py:97
  212.6 2.7 convolution_select_fusion.2
  215.2 2.5 copy.45
  217.8 3.3 fusion.20
  221.1 5.2 conditional.8
  221.1 2.5 copy.61
  226.3 2.1 convert_element_type.48
  228.4 0.0 all-gather.22.cloned.1.call-start
  228.5 0.5 all-gather.22.cloned.1.call-update
  229.0 1.4 gather_fusion.2
  230.4 32.5 %all-to-all-start.3 = ((bf16[16,32,512]{2,1,0:T(8,128)(2,1)}), bf16[16,32,512]{2,1,0:T(8,128)(2,1)}, u32[]{:S(2)}, u32[]{:S(2)}) async-start(bf16[16,32,512]{2,1,0:T(8,128)(2,1)} %gather_fusion.2), calls=%async_computation.3 | async-start | bytes 1048576 | tf_op jit(solution)/shard_map/all_to_all | solution.py:83
  262.9 1.4 gather_fusion.3
  264.3 7.1 %all-to-all-done.3 = bf16[16,32,512]{2,1,0:T(8,128)(2,1)} async-done(((bf16[16,32,512]{2,1,0:T(8,128)(2,1)}), bf16[16,32,512]{2,1,0:T(8,128)(2,1)}, u32[]{:S(2)}, u32[]{:S(2)}) %all-to-all-start.3) | async-done | bytes 524320 | tf_op jit(solution)/shard_map/all_to_all | solution.py:83
  271.3 6.3 %all-to-all-start.4 = ((bf16[16,32,512]{2,1,0:T(8,128)(2,1)}), bf16[16,32,512]{2,1,0:T(8,128)(2,1)}, u32[]{:S(2)}, u32[]{:S(2)}) async-start(bf16[16,32,512]{2,1,0:T(8,128)(2,1)} %gather_fusion.3), calls=%async_computation.4 | async-start | bytes 1048576 | tf_op jit(solution)/shard_map/all_to_all | solution.py:86
  277.6 0.0 all-gather.24.cloned.1.call-start
  277.6 19.4 %all-to-all-done.4 = bf16[16,32,512]{2,1,0:T(8,128)(2,1)} async-done(((bf16[16,32,512]{2,1,0:T(8,128)(2,1)}), bf16[16,32,512]{2,1,0:T(8,128)(2,1)}, u32[]{:S(2)}, u32[]{:S(2)}) %all-to-all-start.4) | async-done | bytes 524320 | tf_op jit(solution)/shard_map/all_to_all | solution.py:86
  297.0 20.9 %all-gather.20.cloned.1.call-done = bf16[8192,512]{1,0:T(8,128)(2,1)} async-done(((bf16[512,512]{1,0:T(8,128)(2,1)}), bf16[8192,512]{1,0:T(8,128)(2,1)}) %all-gather.20.cloned.1.call-update) | async-done | bytes 8388624 | tf_op jit(solution)/shard_map/all_gather | solution.py:27
  317.9 78.5 %all-gather.22.cloned.1.call-done = bf16[8192,512]{1,0:T(8,128)(2,1)} async-done(((bf16[512,512]{1,0:T(8,128)(2,1)}), bf16[8192,512]{1,0:T(8,128)(2,1)}) %all-gather.22.cloned.1.call-update) | async-done | bytes 8388624 | tf_op jit(solution)/shard_map/all_gather | solution.py:27
  396.4 8.5 %conditional.9 = (f32[512,512]{0,1:T(8,128)}) conditional(s32[]{:T(128)} %convert_element_type.42, (f32[512,512]{1,0:T(8,128)}) %conditional.8, (s32[]{:T(128)}, bf16[16,32,512]{2,1,0:T(8,128)(2,1)}, bf16[16,512,512]{2,1,0:T(8,128)(2,1)}, f32[512,512]{1,0:T(8,128)}, s32[]{:T(128)}, /*index=5*/bf16[16,512,512]{2,1,0:T(8,128)(2,1)}, ...), branch_computations={%region_6.7_spmd, %region_7.8_spmd.clone} | conditional | flops 537919488 | bytes 8388740 | solution.py:97
  396.4 2.7 convolution_select_fusion.4
  399.1 2.5 copy.49
  401.6 3.3 fusion.29
  404.9 4.3 conditional.10
  404.9 1.6 copy.63
  409.2 0.9 convert_element_type.49
  410.1 0.0 all-gather.26.cloned.1.call-start
  410.2 0.7 all-gather.26.cloned.1.call-update
  410.9 1.4 gather_fusion.4
  412.3 30.6 %all-to-all-start.5 = ((bf16[16,32,512]{2,1,0:T(8,128)(2,1)}), bf16[16,32,512]{2,1,0:T(8,128)(2,1)S(1)}, u32[]{:S(2)}, u32[]{:S(2)}) async-start(bf16[16,32,512]{2,1,0:T(8,128)(2,1)} %gather_fusion.4), calls=%async_computation.5 | async-start | bytes 1048576 | tf_op jit(solution)/shard_map/all_to_all | solution.py:83
  442.8 1.4 gather_fusion.5
  444.2 8.2 %all-to-all-done.5 = bf16[16,32,512]{2,1,0:T(8,128)(2,1)S(1)} async-done(((bf16[16,32,512]{2,1,0:T(8,128)(2,1)}), bf16[16,32,512]{2,1,0:T(8,128)(2,1)S(1)}, u32[]{:S(2)}, u32[]{:S(2)}) %all-to-all-start.5) | async-done | bytes 524320 | tf_op jit(solution)/shard_map/all_to_all | solution.py:83
  452.4 6.2 %all-to-all-start.6 = ((bf16[16,32,512]{2,1,0:T(8,128)(2,1)}), bf16[16,32,512]{2,1,0:T(8,128)(2,1)S(1)}, u32[]{:S(2)}, u32[]{:S(2)}) async-start(bf16[16,32,512]{2,1,0:T(8,128)(2,1)} %gather_fusion.5), calls=%async_computation.6 | async-start | bytes 1048576 | tf_op jit(solution)/shard_map/all_to_all | solution.py:86
  458.6 19.4 %all-to-all-done.6 = bf16[16,32,512]{2,1,0:T(8,128)(2,1)S(1)} async-done(((bf16[16,32,512]{2,1,0:T(8,128)(2,1)}), bf16[16,32,512]{2,1,0:T(8,128)(2,1)S(1)}, u32[]{:S(2)}, u32[]{:S(2)}) %all-to-all-start.6) | async-done | bytes 524320 | tf_op jit(solution)/shard_map/all_to_all | solution.py:86
  477.9 21.0 %all-gather.24.cloned.1.call-done = bf16[8192,512]{1,0:T(8,128)(2,1)} async-done(((bf16[512,512]{1,0:T(8,128)(2,1)}), bf16[8192,512]{1,0:T(8,128)(2,1)}) %all-gather.24.cloned.1.call-update) | async-done | bytes 8388624 | tf_op jit(solution)/shard_map/all_gather | solution.py:27
  498.9 78.6 %all-gather.26.cloned.1.call-done = bf16[8192,512]{1,0:T(8,128)(2,1)} async-done(((bf16[512,512]{1,0:T(8,128)(2,1)}), bf16[8192,512]{1,0:T(8,128)(2,1)}) %all-gather.26.cloned.1.call-update) | async-done | bytes 8388624 | tf_op jit(solution)/shard_map/all_gather | solution.py:27
  577.6 6.1 %conditional.11 = (f32[512,512]{0,1:T(8,128)}) conditional(s32[]{:T(128)} %convert_element_type.40, (f32[512,512]{1,0:T(8,128)S(1)}) %conditional.10, (s32[]{:T(128)}, bf16[16,512,512]{2,1,0:T(8,128)(2,1)}, bf16[16,32,512]{2,1,0:T(8,128)(2,1)S(1)}, f32[512,512]{1,0:T(8,128)S(1)}, s32[]{:T(128)}, /*index=5*/bf16[16,512,512]{2,1,0:T(8,128)(2,1)}, ...), branch_computations={%region_10.11_spmd, %region_11.12_spmd} | conditional | flops 537919488 | bytes 10485920 | solution.py:97
  577.6 2.7 convolution_select_fusion
  580.3 0.3 copy.53
  580.6 3.0 fusion.11
  583.6 2.5 copy.54
  (17 shorter events, 0.1 us)
Async XLA Ops:
  6.5 48.8 %copy-start = (bf16[1,16,32,512]{3,2,1,0:T(8,128)(2,1)S(1)}, bf16[1,16,32,512]{3,2,1,0:T(8,128)(2,1)}, u32[]{:S(2)}) copy-start(bf16[1,16,32,512]{3,2,1,0:T(8,128)(2,1)} %param.31) | copy-start | bytes 1572868
  6.5 43.0 %all-gather.14.cloned.1.call-start = ((), (), s32[]{:S(2)}) async-start(), calls=%async_computation.7 | async-start | bytes 1114112 | tf_op jit(solution)/shard_map/all_gather | solution.py:49
  12.3 22.7 %all-to-all-start = ((f32[16,1,1,32,512]{4,3,2,1,0:T(8,128)}), f32[16,1,1,32,512]{4,3,2,1,0:T(8,128)S(1)}, u32[]{:S(2)}, u32[]{:S(2)}) async-start(f32[16,1,1,32,512]{4,3,2,1,0:T(8,128)} %broadcast_in_dim.35), calls=%async_computation | async-start | bytes 2097152 | tf_op jit(solution)/shard_map/all_to_all | solution.py:19
  19.8 137.2 %all-gather.18.cloned.1.call-start = ((), (), s32[]{:S(2)}) async-start(), calls=%async_computation.9 | async-start | bytes 8912896 | tf_op jit(solution)/shard_map/all_gather | solution.py:27
  49.5 5.8 copy-start.7
  49.5 40.9 %copy-start.3 = (bf16[16,1,32,512]{3,2,1,0:T(8,128)(2,1)S(1)}, bf16[16,1,32,512]{3,2,1,0:T(8,128)(2,1)}, u32[]{:S(2)}) copy-start(bf16[16,1,32,512]{3,2,1,0:T(8,128)(2,1)} %param.32) | copy-start | bytes 1572868
  52.4 168.7 %copy-start.1 = (f32[1,1,512,512]{3,2,1,0:T(8,128)S(1)}, f32[1,1,512,512]{3,2,1,0:T(8,128)}, u32[]{:S(2)}) copy-start(f32[1,1,512,512]{3,2,1,0:T(8,128)} %all-gather.14.cloned.1.call-done) | copy-start | bytes 3145732
  54.6 158.0 %all-gather.16.cloned.1.call-start = ((), (), s32[]{:S(2)}) async-start(), calls=%async_computation.8 | async-start | bytes 8912896 | tf_op jit(solution)/shard_map/all_gather | solution.py:27
  56.7 43.7 %all-to-all-start.1 = ((bf16[16,32,512]{2,1,0:T(8,128)(2,1)}), bf16[16,32,512]{2,1,0:T(8,128)(2,1)}, u32[]{:S(2)}, u32[]{:S(2)}) async-start(bf16[16,32,512]{2,1,0:T(8,128)(2,1)} %gather_fusion), calls=%async_computation.1 | async-start | bytes 1048576 | tf_op jit(solution)/shard_map/all_to_all | solution.py:83
  100.4 25.1 %all-to-all-start.2 = ((bf16[16,32,512]{2,1,0:T(8,128)(2,1)}), bf16[16,32,512]{2,1,0:T(8,128)(2,1)}, u32[]{:S(2)}, u32[]{:S(2)}) async-start(bf16[16,32,512]{2,1,0:T(8,128)(2,1)} %gather_fusion.1), calls=%async_computation.2 | async-start | bytes 1048576 | tf_op jit(solution)/shard_map/all_to_all | solution.py:86
  110.6 207.4 %all-gather.20.cloned.1.call-start = ((), (), s32[]{:S(2)}) async-start(), calls=%async_computation.10 | async-start | bytes 8912896 | tf_op jit(solution)/shard_map/all_gather | solution.py:27
  221.1 7.9 %copy-start.6 = (s32[16]{0:T(128)S(1)}, s32[16]{0:T(128)}, u32[]{:S(2)}) copy-start(s32[16]{0:T(128)} %constant.202) | copy-start | bytes 196
  228.4 168.0 %all-gather.22.cloned.1.call-start = ((), (), s32[]{:S(2)}) async-start(), calls=%async_computation.11 | async-start | bytes 8912896 | tf_op jit(solution)/shard_map/all_gather | solution.py:27
  230.4 40.9 %all-to-all-start.3 = ((bf16[16,32,512]{2,1,0:T(8,128)(2,1)}), bf16[16,32,512]{2,1,0:T(8,128)(2,1)}, u32[]{:S(2)}, u32[]{:S(2)}) async-start(bf16[16,32,512]{2,1,0:T(8,128)(2,1)} %gather_fusion.2), calls=%async_computation.3 | async-start | bytes 1048576 | tf_op jit(solution)/shard_map/all_to_all | solution.py:83
  271.3 25.7 %all-to-all-start.4 = ((bf16[16,32,512]{2,1,0:T(8,128)(2,1)}), bf16[16,32,512]{2,1,0:T(8,128)(2,1)}, u32[]{:S(2)}, u32[]{:S(2)}) async-start(bf16[16,32,512]{2,1,0:T(8,128)(2,1)} %gather_fusion.3), calls=%async_computation.4 | async-start | bytes 1048576 | tf_op jit(solution)/shard_map/all_to_all | solution.py:86
  277.6 221.3 %all-gather.24.cloned.1.call-start = ((), (), s32[]{:S(2)}) async-start(), calls=%async_computation.12 | async-start | bytes 8912896 | tf_op jit(solution)/shard_map/all_gather | solution.py:27
  404.9 5.9 %copy-start.5 = (s32[16]{0:T(128)S(1)}, s32[16]{0:T(128)}, u32[]{:S(2)}) copy-start(s32[16]{0:T(128)} %constant.218) | copy-start | bytes 196
  410.1 167.4 %all-gather.26.cloned.1.call-start = ((), (), s32[]{:S(2)}) async-start(), calls=%async_computation.13 | async-start | bytes 8912896 | tf_op jit(solution)/shard_map/all_gather | solution.py:27
  412.3 40.1 %all-to-all-start.5 = ((bf16[16,32,512]{2,1,0:T(8,128)(2,1)}), bf16[16,32,512]{2,1,0:T(8,128)(2,1)S(1)}, u32[]{:S(2)}, u32[]{:S(2)}) async-start(bf16[16,32,512]{2,1,0:T(8,128)(2,1)} %gather_fusion.4), calls=%async_computation.5 | async-start | bytes 1048576 | tf_op jit(solution)/shard_map/all_to_all | solution.py:83
  452.4 25.5 %all-to-all-start.6 = ((bf16[16,32,512]{2,1,0:T(8,128)(2,1)}), bf16[16,32,512]{2,1,0:T(8,128)(2,1)S(1)}, u32[]{:S(2)}, u32[]{:S(2)}) async-start(bf16[16,32,512]{2,1,0:T(8,128)(2,1)} %gather_fusion.5), calls=%async_computation.6 | async-start | bytes 1048576 | tf_op jit(solution)/shard_map/all_to_all | solution.py:86
  577.6 2.7 copy-start.4
Sparse Core Ops, SparseCore 0:
  10.5 38.9 all-gather.13
  54.7 102.1 all-gather.17
  158.8 53.7 all-gather.15
  228.5 89.3 all-gather.19
  320.2 76.1 all-gather.21
  410.2 88.6 all-gather.23
  501.3 76.1 all-gather.25
where the time goes:
time: 604 us; the launch traced here: 594 us
  waiting for transfers between devices  394 us (65%)
  starting transfers between devices  127 us (21%)
  local copies, waits for them, and re-layouts  26.1 us (4%)
  matrix products  17.7 us (3%)
  between operations  14.1 us (2%)
  loops' own time  8.24 us (1%)
  other arithmetic  6.23 us (1%)
    all_gather x6, waiting for transfers between devices, broadcast(): lax.all_gather(array, axis)  286 us
    all_to_all x3, starting transfers between devices, per_device(): lax.all_to_all(a_tiles[0, a_rows], 'col', split_axis=0, concat_axis=0, ti...  96.8 us
    all_to_all x3, waiting for transfers between devices, per_device(): lax.all_to_all(b_tiles[b_rows, 0], 'row', split_axis=0, concat_axis=0, ti...  53.6 us
    all_to_all x3, waiting for transfers between devices, per_device(): lax.all_to_all(a_tiles[0, a_rows], 'col', split_axis=0, concat_axis=0, ti...  23.9 us
    all_to_all x3, starting transfers between devices, per_device(): lax.all_to_all(b_tiles[b_rows, 0], 'row', split_axis=0, concat_axis=0, ti...  22.6 us
    all_gather x1, waiting for transfers between devices, per_device(): v_base = lax.all_gather(v_powers[:, :1], 'row', axis=2, tiled=True)[0, 0]  14.5 us
    all_to_all x1, waiting for transfers between devices, from_everyone(): return lax.all_to_all(copies, axis, split_axis=0, concat_axis=0, tiled=True)  14.1 us
  transfers between devices with their start and end apart: 14, of which 14 were waited for; matrix products, arithmetic and copies ran while one was open for 2% of the time, Pallas kernels for 0%

commit v1 on v0

--- a/solution.py
+++ b/solution.py
@@ -46,7 +46,9 @@
     identity = jnp.eye(width, dtype=jnp.float32)
     shift_value = shift[0]
     u_base = gathered_copies(u_powers[:, :1], "col", 2)[0, 0]
-    v_base = lax.all_gather(v_powers[:, :1], "row", axis=2, tiled=True)[0, 0]
+    v_base = jnp.concatenate(
+        lax.all_to_all(jnp.stack([v_powers[:, :1]] * lax.axis_size("row")), "row", 0, 0), axis=2
+    )[0, 0]
 
     def powers_of():
         u_square = product(u_base, u_base)

time: 604 us -> 632 us (1.046)
  waiting for transfers between devices: 394 us -> 421 us
    all_to_all x0 -> x1, waiting for transfers between devices: none -> 23.2 us  [per_device(): lax.all_to_all(jnp.stack([v_powers[:, :1]] * lax.axis_size('row')), 'row'...]
    all_gather x1 -> x0, waiting for transfers between devices: 14.5 us -> none  [per_device(): v_base = lax.all_gather(v_powers[:, :1], 'row', axis=2, tiled=True)[0, 0]]
    all_gather x6, waiting for transfers between devices: 286 us -> 299 us  [broadcast(): lax.all_gather(array, axis)]
    all_to_all x0 -> x1, starting transfers between devices: none -> 8.13 us  [per_device(): lax.all_to_all(jnp.stack([v_powers[:, :1]] * lax.axis_size('row')), 'row'...]
where the time goes in v1:
time: 632 us; the launch traced here: 622 us
  waiting for transfers between devices  421 us (67%)
  starting transfers between devices  128 us (20%)
  local copies, waits for them, and re-layouts  26.5 us (4%)
  matrix products  17.7 us (3%)
  between operations  14.1 us (2%)
  loops' own time  8.23 us (1%)
    all_gather x6, waiting for transfers between devices, broadcast(): lax.all_gather(array, axis)  299 us
    all_to_all x3, starting transfers between devices, per_device(): lax.all_to_all(a_tiles[0, a_rows], 'col', split_axis=0, concat_axis=0, ti...  93.4 us
    all_to_all x3, waiting for transfers between devices, per_device(): lax.all_to_all(b_tiles[b_rows, 0], 'row', split_axis=0, concat_axis=0, ti...  58.1 us
    all_to_all x3, waiting for transfers between devices, per_device(): lax.all_to_all(a_tiles[0, a_rows], 'col', split_axis=0, concat_axis=0, ti...  24.3 us
    all_to_all x1, waiting for transfers between devices, per_device(): lax.all_to_all(jnp.stack([v_powers[:, :1]] * lax.axis_size('row')), 'row'...  23.2 us
    all_to_all x3, starting transfers between devices, per_device(): lax.all_to_all(b_tiles[b_rows, 0], 'row', split_axis=0, concat_axis=0, ti...  19 us
    all_to_all x1, waiting for transfers between devices, from_everyone(): return lax.all_to_all(copies, axis, split_axis=0, concat_axis=0, tiled=True)  14.4 us
  transfers between devices with their start and end apart: 14, of which 14 were waited for; matrix products, arithmetic and copies ran while one was open for 2% of the time, Pallas kernels for 0%

profile of v1, /device:TPU:70, one launch (start us, length us, event | category | flops | bytes accessed | tf_op | source)
XLA Modules:
  0.0 621.9 jit_solution(12713741745803219165)
XLA Ops:
  6.5 2.3 copy.78
  8.9 0.8 slice_bitcast_fusion.1
  9.7 1.1 broadcast_in_dim.35
  10.8 7.4 %all-to-all-start = ((f32[16,1,1,32,512]{4,3,2,1,0:T(8,128)}), f32[16,1,1,32,512]{4,3,2,1,0:T(8,128)S(1)}, u32[]{:S(2)}, u32[]{:S(2)}) async-start(f32[16,1,1,32,512]{4,3,2,1,0:T(8,128)} %broadcast_in_dim.35), calls=%async_computation | async-start | bytes 2097152 | tf_op jit(solution)/shard_map/all_to_all | solution.py:19
  18.2 0.8 slice_bitcast_fusion
  19.1 14.4 %all-to-all-done = f32[16,1,1,32,512]{4,3,2,1,0:T(8,128)S(1)} async-done(((f32[16,1,1,32,512]{4,3,2,1,0:T(8,128)}), f32[16,1,1,32,512]{4,3,2,1,0:T(8,128)S(1)}, u32[]{:S(2)}, u32[]{:S(2)}) %all-to-all-start) | async-done | bytes 1048608 | tf_op jit(solution)/shard_map/all_to_all | solution.py:19
  33.5 1.1 stack.2
  34.6 8.1 %all-to-all-start.1 = ((f32[16,1,1,32,512]{4,3,2,1,0:T(8,128)}), f32[16,1,1,32,512]{4,3,2,1,0:T(8,128)S(1)}, u32[]{:S(2)}, u32[]{:S(2)}) async-start(f32[16,1,1,32,512]{4,3,2,1,0:T(8,128)} %stack.2), calls=%async_computation.1 | async-start | bytes 2097152 | tf_op jit(solution)/shard_map/all_to_all | solution.py:50
  42.7 0.0 all-gather.13.cloned.1.call-start
  42.8 1.1 fusion.36
  43.9 23.2 %all-to-all-done.1 = f32[16,1,1,32,512]{4,3,2,1,0:T(8,128)S(1)} async-done(((f32[16,1,1,32,512]{4,3,2,1,0:T(8,128)}), f32[16,1,1,32,512]{4,3,2,1,0:T(8,128)S(1)}, u32[]{:S(2)}, u32[]{:S(2)}) %all-to-all-start.1) | async-done | bytes 1048608 | tf_op jit(solution)/shard_map/all_to_all | solution.py:50
  67.1 2.9 conditional.6
  70.0 2.1 convert_element_type.47
  72.1 0.0 all-gather.15.cloned.1.call-start
  72.2 0.7 all-gather.15.cloned.1.call-update
  72.9 1.4 gather_fusion
  74.3 31.9 %all-to-all-start.2 = ((bf16[16,32,512]{2,1,0:T(8,128)(2,1)}), bf16[16,32,512]{2,1,0:T(8,128)(2,1)}, u32[]{:S(2)}, u32[]{:S(2)}) async-start(bf16[16,32,512]{2,1,0:T(8,128)(2,1)} %gather_fusion), calls=%async_computation.2 | async-start | bytes 1048576 | tf_op jit(solution)/shard_map/all_to_all | solution.py:85
  106.2 1.4 gather_fusion.1
  107.6 9.4 %all-to-all-done.2 = bf16[16,32,512]{2,1,0:T(8,128)(2,1)} async-done(((bf16[16,32,512]{2,1,0:T(8,128)(2,1)}), bf16[16,32,512]{2,1,0:T(8,128)(2,1)}, u32[]{:S(2)}, u32[]{:S(2)}) %all-to-all-start.2) | async-done | bytes 524320 | tf_op jit(solution)/shard_map/all_to_all | solution.py:85
  116.9 6.1 all-to-all-start.3
  123.0 0.0 all-gather.17.cloned.1.call-start
  123.1 19.4 %all-to-all-done.3 = bf16[16,32,512]{2,1,0:T(8,128)(2,1)} async-done(((bf16[16,32,512]{2,1,0:T(8,128)(2,1)}), bf16[16,32,512]{2,1,0:T(8,128)(2,1)}, u32[]{:S(2)}, u32[]{:S(2)}) %all-to-all-start.3) | async-done | bytes 524320 | tf_op jit(solution)/shard_map/all_to_all | solution.py:88
  142.4 20.4 %all-gather.13.cloned.1.call-done = bf16[8192,512]{1,0:T(8,128)(2,1)} async-done(((bf16[512,512]{1,0:T(8,128)(2,1)}), bf16[8192,512]{1,0:T(8,128)(2,1)}) %all-gather.13.cloned.1.call-update) | async-done | bytes 8388624 | tf_op jit(solution)/shard_map/all_gather | solution.py:27
  162.8 78.6 %all-gather.15.cloned.1.call-done = bf16[8192,512]{1,0:T(8,128)(2,1)} async-done(((bf16[512,512]{1,0:T(8,128)(2,1)}), bf16[8192,512]{1,0:T(8,128)(2,1)}) %all-gather.15.cloned.1.call-update) | async-done | bytes 8388624 | tf_op jit(solution)/shard_map/all_gather | solution.py:27
  241.4 8.5 %conditional.7 = (f32[512,512]{0,1:T(8,128)}) conditional(s32[]{:T(128)} %convert_element_type.44, (f32[512,512]{1,0:T(8,128)}) %conditional.6, (s32[]{:T(128)}, bf16[16,32,512]{2,1,0:T(8,128)(2,1)}, bf16[16,512,512]{2,1,0:T(8,128)(2,1)}, f32[512,512]{1,0:T(8,128)}, s32[]{:T(128)}, /*index=5*/bf16[16,512,512]{2,1,0:T(8,128)(2,1)}, ...), branch_computations={%region_2.3_spmd, %region_3.4_spmd.clone} | conditional | flops 537919488 | bytes 8388740 | solution.py:99
  241.4 2.7 convolution_select_fusion.2
  244.1 2.5 copy.45
  246.6 3.3 fusion.20
  250.0 5.2 conditional.8
  250.0 2.5 copy.61
  255.2 2.1 convert_element_type.48
  257.3 0.0 all-gather.19.cloned.1.call-start
  257.4 0.5 all-gather.19.cloned.1.call-update
  257.9 1.4 gather_fusion.2
  259.3 31.0 %all-to-all-start.4 = ((bf16[16,32,512]{2,1,0:T(8,128)(2,1)}), bf16[16,32,512]{2,1,0:T(8,128)(2,1)}, u32[]{:S(2)}, u32[]{:S(2)}) async-start(bf16[16,32,512]{2,1,0:T(8,128)(2,1)} %gather_fusion.2), calls=%async_computation.4 | async-start | bytes 1048576 | tf_op jit(solution)/shard_map/all_to_all | solution.py:85
  290.2 1.4 gather_fusion.3
  291.6 6.8 %all-to-all-done.4 = bf16[16,32,512]{2,1,0:T(8,128)(2,1)} async-done(((bf16[16,32,512]{2,1,0:T(8,128)(2,1)}), bf16[16,32,512]{2,1,0:T(8,128)(2,1)}, u32[]{:S(2)}, u32[]{:S(2)}) %all-to-all-start.4) | async-done | bytes 524320 | tf_op jit(solution)/shard_map/all_to_all | solution.py:85
  298.4 6.7 %all-to-all-start.5 = ((bf16[16,32,512]{2,1,0:T(8,128)(2,1)}), bf16[16,32,512]{2,1,0:T(8,128)(2,1)}, u32[]{:S(2)}, u32[]{:S(2)}) async-start(bf16[16,32,512]{2,1,0:T(8,128)(2,1)} %gather_fusion.3), calls=%async_computation.5 | async-start | bytes 1048576 | tf_op jit(solution)/shard_map/all_to_all | solution.py:88
  305.1 0.0 all-gather.21.cloned.1.call-start
  305.2 19.4 %all-to-all-done.5 = bf16[16,32,512]{2,1,0:T(8,128)(2,1)} async-done(((bf16[16,32,512]{2,1,0:T(8,128)(2,1)}), bf16[16,32,512]{2,1,0:T(8,128)(2,1)}, u32[]{:S(2)}, u32[]{:S(2)}) %all-to-all-start.5) | async-done | bytes 524320 | tf_op jit(solution)/shard_map/all_to_all | solution.py:88
  324.6 21.9 %all-gather.17.cloned.1.call-done = bf16[8192,512]{1,0:T(8,128)(2,1)} async-done(((bf16[512,512]{1,0:T(8,128)(2,1)}), bf16[8192,512]{1,0:T(8,128)(2,1)}) %all-gather.17.cloned.1.call-update) | async-done | bytes 8388624 | tf_op jit(solution)/shard_map/all_gather | solution.py:27
  346.5 78.5 %all-gather.19.cloned.1.call-done = bf16[8192,512]{1,0:T(8,128)(2,1)} async-done(((bf16[512,512]{1,0:T(8,128)(2,1)}), bf16[8192,512]{1,0:T(8,128)(2,1)}) %all-gather.19.cloned.1.call-update) | async-done | bytes 8388624 | tf_op jit(solution)/shard_map/all_gather | solution.py:27
  425.0 8.5 %conditional.9 = (f32[512,512]{0,1:T(8,128)}) conditional(s32[]{:T(128)} %convert_element_type.42, (f32[512,512]{1,0:T(8,128)}) %conditional.8, (s32[]{:T(128)}, bf16[16,32,512]{2,1,0:T(8,128)(2,1)}, bf16[16,512,512]{2,1,0:T(8,128)(2,1)}, f32[512,512]{1,0:T(8,128)}, s32[]{:T(128)}, /*index=5*/bf16[16,512,512]{2,1,0:T(8,128)(2,1)}, ...), branch_computations={%region_6.7_spmd, %region_7.8_spmd.clone} | conditional | flops 537919488 | bytes 8388740 | solution.py:99
  425.0 2.7 convolution_select_fusion.4
  427.6 2.5 copy.49
  430.2 3.3 fusion.29
  433.5 4.3 conditional.10
  433.5 1.6 copy.63
  437.8 0.9 convert_element_type.49
  438.7 0.0 all-gather.23.cloned.1.call-start
  438.7 0.5 all-gather.23.cloned.1.call-update
  439.3 1.4 gather_fusion.4
  440.7 30.6 %all-to-all-start.6 = ((bf16[16,32,512]{2,1,0:T(8,128)(2,1)}), bf16[16,32,512]{2,1,0:T(8,128)(2,1)S(1)}, u32[]{:S(2)}, u32[]{:S(2)}) async-start(bf16[16,32,512]{2,1,0:T(8,128)(2,1)} %gather_fusion.4), calls=%async_computation.6 | async-start | bytes 1048576 | tf_op jit(solution)/shard_map/all_to_all | solution.py:85
  471.2 1.4 gather_fusion.5
  472.6 8.2 %all-to-all-done.6 = bf16[16,32,512]{2,1,0:T(8,128)(2,1)S(1)} async-done(((bf16[16,32,512]{2,1,0:T(8,128)(2,1)}), bf16[16,32,512]{2,1,0:T(8,128)(2,1)S(1)}, u32[]{:S(2)}, u32[]{:S(2)}) %all-to-all-start.6) | async-done | bytes 524320 | tf_op jit(solution)/shard_map/all_to_all | solution.py:85
  480.8 6.2 all-to-all-start.7
  487.0 19.4 %all-to-all-done.7 = bf16[16,32,512]{2,1,0:T(8,128)(2,1)S(1)} async-done(((bf16[16,32,512]{2,1,0:T(8,128)(2,1)}), bf16[16,32,512]{2,1,0:T(8,128)(2,1)S(1)}, u32[]{:S(2)}, u32[]{:S(2)}) %all-to-all-start.7) | async-done | bytes 524320 | tf_op jit(solution)/shard_map/all_to_all | solution.py:88
  506.4 21.1 %all-gather.21.cloned.1.call-done = bf16[8192,512]{1,0:T(8,128)(2,1)} async-done(((bf16[512,512]{1,0:T(8,128)(2,1)}), bf16[8192,512]{1,0:T(8,128)(2,1)}) %all-gather.21.cloned.1.call-update) | async-done | bytes 8388624 | tf_op jit(solution)/shard_map/all_gather | solution.py:27
  527.5 78.5 %all-gather.23.cloned.1.call-done = bf16[8192,512]{1,0:T(8,128)(2,1)} async-done(((bf16[512,512]{1,0:T(8,128)(2,1)}), bf16[8192,512]{1,0:T(8,128)(2,1)}) %all-gather.23.cloned.1.call-update) | async-done | bytes 8388624 | tf_op jit(solution)/shard_map/all_gather | solution.py:27
  606.0 6.1 conditional.11
  606.0 2.7 convolution_select_fusion
  608.7 0.3 copy.53
  609.0 3.0 fusion.11
  612.0 2.5 copy.54
  (15 shorter events, 0.1 us)
Async XLA Ops:
  6.5 66.3 %copy-start = (bf16[1,16,32,512]{3,2,1,0:T(8,128)(2,1)S(1)}, bf16[1,16,32,512]{3,2,1,0:T(8,128)(2,1)}, u32[]{:S(2)}) copy-start(bf16[1,16,32,512]{3,2,1,0:T(8,128)(2,1)} %param.31) | copy-start | bytes 1572868
  10.8 22.7 %all-to-all-start = ((f32[16,1,1,32,512]{4,3,2,1,0:T(8,128)}), f32[16,1,1,32,512]{4,3,2,1,0:T(8,128)S(1)}, u32[]{:S(2)}, u32[]{:S(2)}) async-start(f32[16,1,1,32,512]{4,3,2,1,0:T(8,128)} %broadcast_in_dim.35), calls=%async_computation | async-start | bytes 2097152 | tf_op jit(solution)/shard_map/all_to_all | solution.py:19
  34.6 32.5 %all-to-all-start.1 = ((f32[16,1,1,32,512]{4,3,2,1,0:T(8,128)}), f32[16,1,1,32,512]{4,3,2,1,0:T(8,128)S(1)}, u32[]{:S(2)}, u32[]{:S(2)}) async-start(f32[16,1,1,32,512]{4,3,2,1,0:T(8,128)} %stack.2), calls=%async_computation.1 | async-start | bytes 2097152 | tf_op jit(solution)/shard_map/all_to_all | solution.py:50
  42.7 120.1 %all-gather.13.cloned.1.call-start = ((), (), s32[]{:S(2)}) async-start(), calls=%async_computation.8 | async-start | bytes 8912896 | tf_op jit(solution)/shard_map/all_gather | solution.py:27
  67.1 5.8 copy-start.5
  67.1 39.0 %copy-start.1 = (bf16[16,1,32,512]{3,2,1,0:T(8,128)(2,1)S(1)}, bf16[16,1,32,512]{3,2,1,0:T(8,128)(2,1)}, u32[]{:S(2)}) copy-start(bf16[16,1,32,512]{3,2,1,0:T(8,128)(2,1)} %param.32) | copy-start | bytes 1572868
  72.1 169.3 %all-gather.15.cloned.1.call-start = ((), (), s32[]{:S(2)}) async-start(), calls=%async_computation.9 | async-start | bytes 8912896 | tf_op jit(solution)/shard_map/all_gather | solution.py:27
  74.3 42.6 %all-to-all-start.2 = ((bf16[16,32,512]{2,1,0:T(8,128)(2,1)}), bf16[16,32,512]{2,1,0:T(8,128)(2,1)}, u32[]{:S(2)}, u32[]{:S(2)}) async-start(bf16[16,32,512]{2,1,0:T(8,128)(2,1)} %gather_fusion), calls=%async_computation.2 | async-start | bytes 1048576 | tf_op jit(solution)/shard_map/all_to_all | solution.py:85
  116.9 25.5 %all-to-all-start.3 = ((bf16[16,32,512]{2,1,0:T(8,128)(2,1)}), bf16[16,32,512]{2,1,0:T(8,128)(2,1)}, u32[]{:S(2)}, u32[]{:S(2)}) async-start(bf16[16,32,512]{2,1,0:T(8,128)(2,1)} %gather_fusion.1), calls=%async_computation.3 | async-start | bytes 1048576 | tf_op jit(solution)/shard_map/all_to_all | solution.py:88
  123.0 223.4 %all-gather.17.cloned.1.call-start = ((), (), s32[]{:S(2)}) async-start(), calls=%async_computation.10 | async-start | bytes 8912896 | tf_op jit(solution)/shard_map/all_gather | solution.py:27
  250.0 7.9 %copy-start.4 = (s32[16]{0:T(128)S(1)}, s32[16]{0:T(128)}, u32[]{:S(2)}) copy-start(s32[16]{0:T(128)} %constant.202) | copy-start | bytes 196
  257.3 167.7 %all-gather.19.cloned.1.call-start = ((), (), s32[]{:S(2)}) async-start(), calls=%async_computation.11 | async-start | bytes 8912896 | tf_op jit(solution)/shard_map/all_gather | solution.py:27
  259.3 39.1 %all-to-all-start.4 = ((bf16[16,32,512]{2,1,0:T(8,128)(2,1)}), bf16[16,32,512]{2,1,0:T(8,128)(2,1)}, u32[]{:S(2)}, u32[]{:S(2)}) async-start(bf16[16,32,512]{2,1,0:T(8,128)(2,1)} %gather_fusion.2), calls=%async_computation.4 | async-start | bytes 1048576 | tf_op jit(solution)/shard_map/all_to_all | solution.py:85
  298.4 26.2 %all-to-all-start.5 = ((bf16[16,32,512]{2,1,0:T(8,128)(2,1)}), bf16[16,32,512]{2,1,0:T(8,128)(2,1)}, u32[]{:S(2)}, u32[]{:S(2)}) async-start(bf16[16,32,512]{2,1,0:T(8,128)(2,1)} %gather_fusion.3), calls=%async_computation.5 | async-start | bytes 1048576 | tf_op jit(solution)/shard_map/all_to_all | solution.py:88
  305.1 222.3 %all-gather.21.cloned.1.call-start = ((), (), s32[]{:S(2)}) async-start(), calls=%async_computation.12 | async-start | bytes 8912896 | tf_op jit(solution)/shard_map/all_gather | solution.py:27
  433.5 5.8 copy-start.3
  438.7 167.3 %all-gather.23.cloned.1.call-start = ((), (), s32[]{:S(2)}) async-start(), calls=%async_computation.13 | async-start | bytes 8912896 | tf_op jit(solution)/shard_map/all_gather | solution.py:27
  440.7 40.2 %all-to-all-start.6 = ((bf16[16,32,512]{2,1,0:T(8,128)(2,1)}), bf16[16,32,512]{2,1,0:T(8,128)(2,1)S(1)}, u32[]{:S(2)}, u32[]{:S(2)}) async-start(bf16[16,32,512]{2,1,0:T(8,128)(2,1)} %gather_fusion.4), calls=%async_computation.6 | async-start | bytes 1048576 | tf_op jit(solution)/shard_map/all_to_all | solution.py:85
  480.8 25.5 %all-to-all-start.7 = ((bf16[16,32,512]{2,1,0:T(8,128)(2,1)}), bf16[16,32,512]{2,1,0:T(8,128)(2,1)S(1)}, u32[]{:S(2)}, u32[]{:S(2)}) async-start(bf16[16,32,512]{2,1,0:T(8,128)(2,1)} %gather_fusion.5), calls=%async_computation.7 | async-start | bytes 1048576 | tf_op jit(solution)/shard_map/all_to_all | solution.py:88
  606.0 2.7 copy-start.2
Sparse Core Ops, SparseCore 0:
  72.2 90.5 all-gather.12
  165.2 76.1 all-gather.14
  257.4 88.9 all-gather.16
  348.7 76.1 all-gather.18
  438.8 88.6 all-gather.20
  529.8 76.1 all-gather.22
